TPU v7x, 256 devices: a whole 4x4x8 slice. The times are simulated.
256 devices in a mesh: dp: 64 (over z, y, core), mp: 4 (over x).
Axes of the slice: x: 4, y: 4, z: 8, core: 2. Of those that a mesh axis runs over, the one named last changes fastest.
Arguments:
- noise_blocks: bfloat16 [512, 12800], P('dp'), may hold values from -6 to 6
- data_blocks: bfloat16 [512, 12800], P('dp'), may hold values from -6 to 6
- destination: int32 [512], replicated, may hold values from 0 to 511, as said below
- utt_blocks: int32 [64, 4], P('dp'), may hold values from 1 to 4, 8 in all within a row
- span_start: int32 [64, 4], P('dp'), may hold values from 0 to 19
- span_size: int32 [64, 4], P('dp'), may hold values from 44 to 64
- timestep: int32 [64, 4], P('dp'), may hold values from 1 to 63
- in_weight: bfloat16 [200, 1024], replicated, may hold values from -0.4375 to 0.4375
- norm_gain: bfloat16 [1024], replicated, may hold values from 0.5 to 1.5
- qkv_weight: bfloat16 [1024, 3, 512], P(None, None, 'mp'), may hold values from -4 to 4
- out_proj: bfloat16 [512, 1024], P('mp'), may hold values from -0.25 to 0.25
- final_gain: bfloat16 [1024], replicated, may hold values from 0.25 to 1.75
- vel_weight: bfloat16 [1024, 100], replicated, may hold values from -0.1875 to 0.1875
Outputs:
- grad_qkv: float32 [1024, 3, 512], P('dp', None, 'mp')
- grad_out: float32 [512, 1024], P('mp', 'dp')
Inputs may be any that keep to these rules, and one draw needn't show every extreme that they name: `destination`: A permutation of the 512 bin positions; a device sends to each bin either none or exactly 1 of its blocks.
All inputs are finite; a program needn't handle non-finite values.
Results may differ from a plain program's by a relative error of at most 0.004.
Values may be sent and summed in bfloat16 or wider, within the bound.
No kernel may reach another device: no remote copies, remote signals or barrier semaphores. Data moves between devices by JAX's collectives and lax.ppermute only.
A program may use at most 64 MiB of HBM per device.

v0:
```python
import jax
import jax.numpy as jnp
from jax import lax
from jax.sharding import PartitionSpec as P

HEAD_DIM = 64
BLOCK = 128


def sent_together(arrays, axis, split_dim, concat_dim, along):
    widths = [a.shape[along] for a in arrays]
    both = jnp.concatenate(arrays, axis=along)
    out = lax.all_to_all(both, axis, split_axis=split_dim, concat_axis=concat_dim, tiled=True)
    return tuple(jnp.split(out, [sum(widths[:k]) for k in range(1, len(widths))], axis=along))


def sent_together_2(arrays, axis, dim, along):
    both = jnp.concatenate(arrays, axis=along)
    out, at, finished = (lax.all_gather(both, axis, axis=dim, tiled=True), 0, [])
    for a in arrays:
        finished.append(lax.slice_in_dim(out, at, at + a.shape[along], axis=along))
        at += a.shape[along]
    return tuple(finished)


def sent_to_all(shard, axis):
    length = lax.axis_size(axis)
    return lax.all_to_all(
        jnp.broadcast_to(shard[None], (length, *shard.shape)), axis, 0, 0, tiled=True
    )


def of_everyone(shard, axis):
    return sent_to_all(shard, axis).sum(axis=0)


def split_up(shard, dim, length):
    dims = shard.shape
    tiles = shard.reshape(*dims[:dim], length, dims[dim] // length, *dims[dim + 1 :])
    return jnp.moveaxis(tiles, dim, 0)


def sent_and_summed(shard, axis, dim):
    length = lax.axis_size(axis)
    tiles = lax.all_to_all(split_up(shard, dim, length), axis, 0, 0, tiled=True)
    return jnp.sum(tiles, axis=0)


def frame_table(lengths, starts, sizes, steps, rows):
    ends = jnp.cumsum(lengths)
    frame = jnp.arange(rows, dtype=jnp.int32)
    block_index = frame // BLOCK
    segment = jnp.sum((block_index[:, None] >= ends[None, :]).astype(jnp.int32), axis=1)
    member = segment[:, None] == jnp.arange(lengths.shape[0], dtype=jnp.int32)[None, :]
    first = jnp.sum(jnp.where(member, (ends - lengths)[None, :], 0), axis=1) * BLOCK
    span = jnp.sum(jnp.where(member, lengths[None, :], 0), axis=1) * BLOCK
    lower = jnp.sum(jnp.where(member, starts[None, :], 0), axis=1)
    upper = lower + jnp.sum(jnp.where(member, sizes[None, :], 0), axis=1)
    inside = 64 * (frame - first)
    masked = ((inside >= lower * span) & (inside < upper * span)).astype(jnp.float32)
    level = jnp.sum(jnp.where(member, steps[None, :], 0), axis=1).astype(jnp.float32) / 64.0
    return (segment, masked, level)


def attend(query, keys, values, segment):
    rows, width = query.shape
    heads = width // HEAD_DIM
    block = min(512, rows)
    reach = min(4, rows // BLOCK // 2) * BLOCK
    window = min(rows, block + 2 * reach)
    blocks = rows // block
    query_blocks = query.reshape(blocks, block, heads, HEAD_DIM)
    segment_blocks = segment.reshape(blocks, block)
    firsts = jnp.clip(jnp.arange(blocks, dtype=jnp.int32) * block - reach, 0, rows - window)
    keyed = keys.reshape(rows, heads, HEAD_DIM)
    valued = values.reshape(rows, heads, HEAD_DIM)

    def one_block(item):
        query_block, segment_block, first = item
        scores = jnp.einsum(
            "qhd,khd->hqk", query_block, keyed, preferred_element_type=jnp.float32
        ) * HEAD_DIM ** (-0.5)
        scores = jnp.where((segment_block[:, None] == segment[None, :])[None], scores, -1e30)
        top = jnp.max(scores, axis=-1, keepdims=True)
        weights = jnp.exp(scores - top)
        probs = (weights / jnp.sum(weights, axis=-1, keepdims=True)).astype(jnp.bfloat16)
        return jnp.einsum(
            "hqk,khd->qhd", probs, valued, preferred_element_type=jnp.float32
        ).reshape(block, width)

    return lax.map(jax.checkpoint(one_block), (query_blocks, segment_blocks, firsts)).reshape(
        rows, width
    )


def shards(
    noise_blocks,
    data_blocks,
    destination,
    utt_blocks,
    span_start,
    span_size,
    timestep,
    in_weight,
    norm_gain,
    qkv_weight,
    out_proj,
    final_gain,
    vel_weight,
):
    sources = lax.axis_size("dp")
    here = lax.axis_index("dp")
    per_dev = noise_blocks.shape[0]
    depth = max(1, per_dev // sources)
    lanes_total = sources * depth
    table = destination.reshape(sources, per_dev)
    owner = table // per_dev
    order = jnp.arange(per_dev, dtype=jnp.int32)
    earlier = (owner[:, :, None] == owner[:, None, :]) & (
        order[None, None, :] < order[None, :, None]
    )
    rank = jnp.sum(earlier.astype(jnp.int32), axis=2)
    code = jnp.arange(sources, dtype=jnp.int32)[:, None] * depth + rank
    mine_owner = lax.dynamic_index_in_dim(owner, here, 0, keepdims=False)
    mine_rank = lax.dynamic_index_in_dim(rank, here, 0, keepdims=False)
    lanes = jnp.arange(lanes_total, dtype=jnp.int32)
    packing = (lanes[:, None] == (mine_owner * depth + mine_rank)[None, :]).astype(jnp.bfloat16)
    wanted = here * per_dev + order
    hit = table[None, :, :] == wanted[:, None, None]
    source_code = jnp.sum(jnp.where(hit, code[None, :, :], 0), axis=(1, 2))
    unpacking = (source_code[:, None] == lanes[None, :]).astype(jnp.bfloat16)

    def outgoing(blocks):
        sent = jnp.dot(packing, blocks, preferred_element_type=jnp.float32).astype(jnp.bfloat16)
        return sent.reshape(sources, depth, blocks.shape[1])

    def incoming(arrived):
        flat = arrived.reshape(lanes_total, arrived.shape[2])
        return jnp.dot(unpacking, flat, preferred_element_type=jnp.float32).astype(jnp.bfloat16)

    share = noise_blocks.shape[1] // lax.axis_size("mp")
    offset = lax.axis_index("mp") * share
    noise_share = lax.dynamic_slice_in_dim(noise_blocks, offset, share, 1)
    data_share = lax.dynamic_slice_in_dim(data_blocks, offset, share, 1)
    got_noise, got_data = sent_together(
        (outgoing(noise_share), outgoing(data_share)), "dp", 0, 0, 1
    )
    bin_noise, bin_data = sent_together_2((incoming(got_noise), incoming(got_data)), "mp", 1, 0)
    rows = per_dev * BLOCK
    mel = noise_blocks.shape[1] // BLOCK
    noise = bin_noise.reshape(rows, mel).astype(jnp.float32)
    data = bin_data.reshape(rows, mel).astype(jnp.float32)
    segment, masked, level = frame_table(
        utt_blocks[0], span_start[0], span_size[0], timestep[0], rows
    )
    noisy = (1.0 - level[:, None]) * noise + level[:, None] * data
    cond = data * (1.0 - masked[:, None])
    target = data - noise
    inputs = jnp.concatenate([noisy, cond], axis=1).astype(jnp.bfloat16)
    hidden0 = jnp.dot(inputs, in_weight, preferred_element_type=jnp.float32)
    scale = lax.rsqrt(jnp.mean(hidden0 * hidden0, axis=1, keepdims=True) + 1e-06)
    normed = (hidden0 * scale * norm_gain.astype(jnp.float32)[None, :]).astype(jnp.bfloat16)
    query = jnp.dot(normed, qkv_weight[:, 0, :], preferred_element_type=jnp.float32).astype(
        jnp.bfloat16
    )
    keys = jnp.dot(normed, qkv_weight[:, 1, :], preferred_element_type=jnp.float32).astype(
        jnp.bfloat16
    )
    values = jnp.dot(normed, qkv_weight[:, 2, :], preferred_element_type=jnp.float32).astype(
        jnp.bfloat16
    )
    heads_out, pullback = jax.vjp(lambda a, b, c: attend(a, b, c, segment), query, keys, values)
    attended = heads_out.astype(jnp.bfloat16)
    partial_mix = jnp.dot(attended, out_proj, preferred_element_type=jnp.float32)
    mixed = lax.psum(partial_mix.astype(jnp.bfloat16), "mp").astype(jnp.float32)
    hidden1 = (hidden0 + mixed).astype(jnp.bfloat16)
    wide1 = lax.optimization_barrier(hidden1).astype(jnp.float32)
    rscale = lax.rsqrt(jnp.mean(wide1 * wide1, axis=1, keepdims=True) + 1e-06)
    normalized = wide1 * rscale
    gain_out = final_gain.astype(jnp.float32)[None, :]
    final = (normalized * gain_out).astype(jnp.bfloat16)
    velocity = jnp.dot(final, vel_weight, preferred_element_type=jnp.float32)
    count = of_everyone(jnp.sum(masked), "dp")
    error = (2.0 * masked[:, None] * (velocity - target)).astype(jnp.bfloat16)
    grad_final = jnp.dot(error, vel_weight.T, preferred_element_type=jnp.float32)
    scaled = grad_final * gain_out
    back1 = (
        rscale * (scaled - normalized * jnp.mean(scaled * normalized, axis=1, keepdims=True))
    ).astype(jnp.bfloat16)
    back_att = jnp.dot(back1, out_proj.T, preferred_element_type=jnp.float32).astype(jnp.bfloat16)
    dquery, dkeys, dvalues = pullback(back_att.astype(jnp.float32))
    out_terms = jnp.dot(attended.T, back1, preferred_element_type=jnp.float32)
    qkv_terms = jnp.stack(
        [
            jnp.dot(normed.T, dquery, preferred_element_type=jnp.float32),
            jnp.dot(normed.T, dkeys, preferred_element_type=jnp.float32),
            jnp.dot(normed.T, dvalues, preferred_element_type=jnp.float32),
        ],
        axis=1,
    )
    summed_qkv, summed_out = (
        sent_and_summed(qkv_terms, "dp", 0),
        sent_and_summed(out_terms, "dp", 1),
    )
    return (summed_qkv / count, summed_out / count)


def solution(mesh):
    in_specs = (
        P("dp", None),
        P("dp", None),
        P(),
        P("dp", None),
        P("dp", None),
        P("dp", None),
        P("dp", None),
        P(),
        P(),
        P(None, None, "mp"),
        P("mp", None),
        P(),
        P(),
    )
    out_specs = (P("dp", None, "mp"), P("mp", "dp"))
    return jax.shard_map(shards, mesh=mesh, in_specs=in_specs, out_specs=out_specs, check_vma=False)
```

profile of v0, /device:TPU:1, one launch (start us, length us, event | category | flops | bytes accessed | tf_op | source)
XLA Modules:
  0.0 277.2 jit_solution(8119586240358613834)
XLA Ops:
  10.7 1.7 copy.118
  12.4 13.2 %all-to-all-start = ((bf16[64,2,3200]{2,1,0:T(2,128)(2,1)}), bf16[64,2,3200]{2,1,0:T(2,128)(2,1)S(1)}, u32[]{:S(2)}, u32[]{:S(2)}) async-start(bf16[64,2,3200]{2,1,0:T(2,128)(2,1)} %copy.118), calls=%async_computation | async-start | bytes 1638400 | tf_op jit(solution)/shard_map/all_to_all | solution.py:13
  27.7 21.2 %all-to-all-done = bf16[64,2,3200]{2,1,0:T(2,128)(2,1)S(1)} async-done(((bf16[64,2,3200]{2,1,0:T(2,128)(2,1)}), bf16[64,2,3200]{2,1,0:T(2,128)(2,1)S(1)}, u32[]{:S(2)}, u32[]{:S(2)}) %all-to-all-start) | async-done | bytes 819232 | tf_op jit(solution)/shard_map/all_to_all | solution.py:13
  48.9 1.1 fusion.127
  50.5 11.4 %all_gather.3 = bf16[16,12800]{1,0:T(8,128)(2,1)S(1)} all-gather(bf16[16,3200]{1,0:T(8,128)(2,1)S(1)} %pad_maximum_fusion.2), channel_id=1, replica_groups=mesh['dp'=64,'mp'=4] {'mp'}, dimensions={1}, use_global_device_ids=true | all-gather | bytes 512000 | tf_op jit(solution)/shard_map/all_gather | solution.py:19
  65.7 1.3 copy-done.27
  70.4 16.2 %while.30 = (s32[]{:T(128)}, bf16[2,512,128]{2,1,0:T(8,128)(2,1)S(1)}, s32[2,512]{1,0:T(2,128)S(1)}, s32[1,1024]{1,0:T(1,128)S(1)}, bf16[2,512,2,64]{1,3,2,0:T(8...) while((s32[]{:T(128)}, ...), condition=%wide.region_13.14_spmd, body=%wide.region_10.13_spmd.sunk | while | flops 275252224 | bytes 10766441 | solution.py:91
  70.7 4.5 %fusion.178 = (f32[2,512]{1,0:T(2,128)S(1)}, f32[2,512,1024]{2,1,0:T(8,128)}) fusion(pred[512,1024]{1,0:T(8,128)(4,1)S(1)} %broadcast_compare_fusion.4, bf16[1024,2,64]{0,2,1:T(8,128)(2,1)S(1)} %get-tuple-element.655, bf16[2,512,2,64]{1,3,2,0:T(8,128)(2,1)} %get-tuple-element.654, s32[]{:T(128)S(6)} %copy.175), kind=kOutput, calls=%fused_computation.183.clone.1 | convolution fusion | flops 138413056 | bytes 5115908 | tf_op jit(solution)/shard_map/jvp()/while/body/eval_jaxpr/sub | solution.py:85
  75.2 3.0 %fusion.179 = bf16[2,512,64]{1,2,0:T(8,128)(2,1)S(1)} fusion(bf16[1024,2,64]{0,2,1:T(8,128)(2,1)S(1)} %get-tuple-element.656, f32[2,512,1024]{2,1,0:T(8,128)} %get-tuple-element.608, f32[2,512]{1,0:T(2,128)S(1)} %get-tuple-element.609), kind=kOutput, calls=%fused_computation.8.clone.1 | convolution fusion | flops 136314880 | bytes 4591616 | tf_op jit(solution)/shard_map/jvp()/while/body/eval_jaxpr/hqk,khd->qhd/dot_general | solution.py:87
  78.8 4.5 %fusion.178 = (f32[2,512]{1,0:T(2,128)S(1)}, f32[2,512,1024]{2,1,0:T(8,128)}) fusion(pred[512,1024]{1,0:T(8,128)(4,1)S(1)} %broadcast_compare_fusion.4, bf16[1024,2,64]{0,2,1:T(8,128)(2,1)S(1)} %get-tuple-element.655, bf16[2,512,2,64]{1,3,2,0:T(8,128)(2,1)} %get-tuple-element.654, s32[]{:T(128)S(6)} %copy.175), kind=kOutput, calls=%fused_computation.183.clone.1 | convolution fusion | flops 138413056 | bytes 5115908 | tf_op jit(solution)/shard_map/jvp()/while/body/eval_jaxpr/sub | solution.py:85
  83.3 3.0 %fusion.179 = bf16[2,512,64]{1,2,0:T(8,128)(2,1)S(1)} fusion(bf16[1024,2,64]{0,2,1:T(8,128)(2,1)S(1)} %get-tuple-element.656, f32[2,512,1024]{2,1,0:T(8,128)} %get-tuple-element.608, f32[2,512]{1,0:T(2,128)S(1)} %get-tuple-element.609), kind=kOutput, calls=%fused_computation.8.clone.1 | convolution fusion | flops 136314880 | bytes 4591616 | tf_op jit(solution)/shard_map/jvp()/while/body/eval_jaxpr/hqk,khd->qhd/dot_general | solution.py:87
  86.6 2.1 convolution_convert_fusion.5
  88.7 1.3 broadcast_in_dim.203
  90.0 8.7 %all-to-all-start.2 = ((f32[64,1,1]{2,1,0:T(1,128)}), f32[64,1,1]{2,1,0:T(1,128)}, u32[]{:S(2)}, u32[]{:S(2)}) async-start(f32[64,1,1]{2,1,0:T(1,128)} %broadcast_in_dim.203), calls=%async_computation.2 | async-start | bytes 65536 | tf_op jit(solution)/shard_map/all_to_all | solution.py:28
  101.4 49.6 %all-reduce.2.cloned.1.call-done = bf16[1024,1024]{0,1:T(8,128)(2,1)} async-done(((bf16[1024,1024]{0,1:T(8,128)(2,1)}), bf16[1024,1024]{0,1:T(8,128)(2,1)}) %all-reduce.2.cloned.1.call-update) | async-done | bytes 2097168 | tf_op jit(solution)/shard_map/psum | solution.py:175
  151.0 3.6 %add_convert_fusion = bf16[1024,1024]{0,1:T(8,128)(2,1)S(1)} fusion(f32[1024,1024]{0,1:T(8,128)} %copy-done.1, bf16[1024,1024]{0,1:T(8,128)(2,1)} %all-reduce.2.cloned.1.call-done), kind=kLoop, calls=%fused_computation.86 | loop fusion | flops 3145728 | bytes 8388608 | tf_op jit(solution)/shard_map/convert_element_type | solution.py:176
  155.1 4.4 %fusion.64 = (f32[1024]{0:T(1024)S(1)}, f32[1024,1024]{0,1:T(8,128)}) fusion(bf16[1024,1024]{0,1:T(8,128)(2,1)S(1)} %add_convert_fusion, f32[1024]{0:T(1024)S(1)} %copy-done.19, f32[1024]{0:T(1024)S(1)} %add_rsqrt_fusion, bf16[1024,100]{0,1:T(8,128)(2,1)} %param.29, f32[1024,100]{0,1:T(8,128)S(1)} %copy-done.10, f32[1024,100]{0,1:T(8,128)S(1)} %copy-done.9, ...), kind=kOutput, calls=%fused_computation.81 | convolution fusion | flops 429276160 | bytes 7331840 | tf_op jit(solution)/shard_map/dot_general | solution.py:185
  159.5 3.2 %fusion.67 = bf16[1024,1024]{0,1:T(8,128)(2,1)S(1)} fusion(bf16[1024,1024]{0,1:T(8,128)(2,1)S(1)} %add_convert_fusion, f32[1024,1024]{0,1:T(8,128)} %get-tuple-element.497, f32[1024]{0:T(1024)S(1)} %broadcast_multiply_fusion, f32[1024]{0:T(1024)S(1)} %copy-done.19, f32[1024]{0:T(1024)S(1)} %add_rsqrt_fusion), kind=kLoop, calls=%fused_computation.84 | loop fusion | flops 7340032 | bytes 8400896 | tf_op jit(solution)/shard_map/convert_element_type | solution.py:189
  162.7 2.3 fusion.75
  165.8 1.1 copy.136
  166.9 10.9 %all-to-all-start.3 = ((f32[64,128,16]{1,2,0:T(8,128)}), f32[64,128,16]{1,2,0:T(8,128)}, u32[]{:S(2)}, u32[]{:S(2)}) async-start(f32[64,128,16]{1,2,0:T(8,128)} %copy.136), calls=%async_computation.3 | async-start | bytes 1048576 | tf_op jit(solution)/shard_map/all_to_all | solution.py:45
  178.5 33.6 %while.31 = (s32[]{:T(128)}, bf16[1024,2,64]{0,2,1:T(8,128)(2,1)}, bf16[1024,2,64]{0,2,1:T(8,128)(2,1)}, bf16[2,512,2,64]{1,3,2,0:T(8,128)(2,1)}, bf16[2,512,2,6...) while((s32[]{:T(128)}, bf16[1024,2,64]{0,2,1:T(8,128)(2,1)}, ...), condition=%wide.region_23.24_spmd.clone, body=%wide.region_17.23_spmd.clone.sunk | while | flops 712179712 | bytes 56854912 | solution.py:91
  178.5 1.4 constant_dynamic-slice_fusion.7
  182.1 2.1 fusion.187
  184.2 1.2 fusion.188
  185.4 1.5 fusion.191
  186.9 2.8 convert_reduce_fusion.5
  189.7 1.9 fusion.189
  191.6 1.5 fusion.190
  193.2 1.5 fusion.192
  195.4 1.3 constant_dynamic-slice_fusion.7
  198.8 2.1 fusion.187
  200.9 1.2 fusion.188
  202.1 1.5 fusion.191
  203.6 2.8 convert_reduce_fusion.5
  206.4 1.9 fusion.189
  208.4 1.5 fusion.190
  209.9 1.5 fusion.192
  212.2 1.2 copy.129
  214.3 1.7 convolution_bitcast_fusion.1
  216.0 1.7 convolution_bitcast_fusion.2
  218.5 1.3 copy.133
  219.7 10.3 %all-to-all-start.1 = ((f32[64,16,3,128]{3,1,2,0:T(8,128)}), f32[64,16,3,128]{3,1,2,0:T(8,128)S(1)}, u32[]{:S(2)}, u32[]{:S(2)}) async-start(f32[64,16,3,128]{3,1,2,0:T(8,128)} %copy.133), calls=%async_computation.1 | async-start | bytes 3145728 | tf_op jit(solution)/shard_map/all_to_all | solution.py:45
  230.0 1.4 reduce_sum.227
  231.5 1.1 reduce_sum.228
  232.6 1.2 broadcast_divide_fusion.1
  233.8 35.2 %all-to-all-done.1 = f32[64,16,3,128]{3,1,2,0:T(8,128)S(1)} async-done(((f32[64,16,3,128]{3,1,2,0:T(8,128)}), f32[64,16,3,128]{3,1,2,0:T(8,128)S(1)}, u32[]{:S(2)}, u32[]{:S(2)}) %all-to-all-start.1) | async-done | bytes 1572896 | tf_op jit(solution)/shard_map/all_to_all | solution.py:45
  269.1 1.2 broadcast_divide_fusion
  (157 shorter events, 26.2 us)
Async XLA Ops:
  7.2 57.2 %copy-start = (bf16[200,1024]{1,0:T(8,128)(2,1)S(1)}, bf16[200,1024]{1,0:T(8,128)(2,1)}, u32[]{:S(2)}) copy-start(bf16[200,1024]{1,0:T(8,128)(2,1)} %param.24) | copy-start | bytes 1228804
  7.2 18.5 %copy-start.24 = (s32[1,4]{1,0:T(1,128)S(1)}, s32[1,4]{1,0:T(1,128)}, u32[]{:S(2)}) copy-start(s32[1,4]{1,0:T(1,128)} %param.20) | copy-start | bytes 52
  7.2 18.6 %copy-start.21 = (bf16[1024]{0:T(1024)(128)(2,1)S(1)}, bf16[1024]{0:T(1024)(128)(2,1)}, u32[]{:S(2)}) copy-start(bf16[1024]{0:T(1024)(128)(2,1)} %param.25) | copy-start | bytes 6148
  7.2 19.1 %copy-start.23 = (s32[1,4]{1,0:T(1,128)S(1)}, s32[1,4]{1,0:T(1,128)}, u32[]{:S(2)}) copy-start(s32[1,4]{1,0:T(1,128)} %param.23) | copy-start | bytes 52
  7.2 19.1 %copy-start.25 = (s32[1,4]{1,0:T(1,128)S(1)}, s32[1,4]{1,0:T(1,128)}, u32[]{:S(2)}) copy-start(s32[1,4]{1,0:T(1,128)} %param.22) | copy-start | bytes 52
  7.2 19.1 %copy-start.26 = (s32[1,4]{1,0:T(1,128)S(1)}, s32[1,4]{1,0:T(1,128)}, u32[]{:S(2)}) copy-start(s32[1,4]{1,0:T(1,128)} %param.21) | copy-start | bytes 52
  12.4 36.5 %all-to-all-start = ((bf16[64,2,3200]{2,1,0:T(2,128)(2,1)}), bf16[64,2,3200]{2,1,0:T(2,128)(2,1)S(1)}, u32[]{:S(2)}, u32[]{:S(2)}) async-start(bf16[64,2,3200]{2,1,0:T(2,128)(2,1)} %copy.118), calls=%async_computation | async-start | bytes 1638400 | tf_op jit(solution)/shard_map/all_to_all | solution.py:13
  25.6 125.4 %all-reduce.2.cloned.1.call-start = ((), (), s32[]{:S(2)}) async-start(), calls=%async_computation.4 | async-start | bytes 4194304 | tf_op jit(solution)/shard_map/psum | solution.py:175
  65.2 2.2 copy-start.1
  65.2 1.7 copy-start.27
  66.9 1.4 copy-start.2
  70.4 16.2 %copy-start.4 = (bf16[128,1024]{1,0:T(8,128)(2,1)S(1)}, bf16[128,1024]{1,0:T(8,128)(2,1)}, u32[]{:S(2)}) copy-start(bf16[128,1024]{1,0:T(8,128)(2,1)} %param.27) | copy-start | bytes 786436
  86.5 14.8 %copy-start.8 = (s32[1,1024]{1,0:T(1,128)}, s32[1,1024]{1,0:T(1,128)S(1)}, u32[]{:S(2)}) copy-start(s32[1,1024]{1,0:T(1,128)S(1)} %get-tuple-element.700) | copy-start | bytes 12292
  86.5 14.8 %copy-start.11 = (bf16[2,512,128]{2,1,0:T(8,128)(2,1)}, bf16[2,512,128]{2,1,0:T(8,128)(2,1)S(1)}, u32[]{:S(2)}) copy-start(bf16[2,512,128]{2,1,0:T(8,128)(2,1)S(1)} %get-tuple-element.271) | copy-start | bytes 786436
  86.5 14.8 %copy-start.18 = (s32[2,512]{1,0:T(2,128)}, s32[2,512]{1,0:T(2,128)S(1)}, u32[]{:S(2)}) copy-start(s32[2,512]{1,0:T(2,128)S(1)} %get-tuple-element.701) | copy-start | bytes 12292
  86.6 14.8 %copy-start.28 = (bf16[1024,2,64]{0,2,1:T(8,128)(2,1)}, bf16[1024,2,64]{0,2,1:T(8,128)(2,1)S(1)}, u32[]{:S(2)}) copy-start(bf16[1024,2,64]{0,2,1:T(8,128)(2,1)S(1)} %get-tuple-element.702) | copy-start | bytes 786436
  86.6 14.8 %copy-start.30 = (bf16[1024,2,64]{0,2,1:T(8,128)(2,1)}, bf16[1024,2,64]{0,2,1:T(8,128)(2,1)S(1)}, u32[]{:S(2)}) copy-start(bf16[1024,2,64]{0,2,1:T(8,128)(2,1)S(1)} %get-tuple-element.703) | copy-start | bytes 786436
  86.6 12.2 %copy-start.22 = (bf16[1024]{0:T(1024)(128)(2,1)S(1)}, bf16[1024]{0:T(1024)(128)(2,1)}, u32[]{:S(2)}) copy-start(bf16[1024]{0:T(1024)(128)(2,1)} %param.28) | copy-start | bytes 6148
  90.0 76.9 %all-to-all-start.2 = ((f32[64,1,1]{2,1,0:T(1,128)}), f32[64,1,1]{2,1,0:T(1,128)}, u32[]{:S(2)}, u32[]{:S(2)}) async-start(f32[64,1,1]{2,1,0:T(1,128)} %broadcast_in_dim.203), calls=%async_computation.2 | async-start | bytes 65536 | tf_op jit(solution)/shard_map/all_to_all | solution.py:28
  101.3 53.8 %copy-start.9 = (f32[1024,100]{0,1:T(8,128)S(1)}, f32[1024,100]{0,1:T(8,128)}, u32[]{:S(2)}) copy-start(f32[1024,100]{0,1:T(8,128)} %copy.126) | copy-start | bytes 1228804
  101.3 53.8 %copy-start.10 = (f32[1024,100]{0,1:T(8,128)S(1)}, f32[1024,100]{0,1:T(8,128)}, u32[]{:S(2)}) copy-start(f32[1024,100]{0,1:T(8,128)} %copy.125) | copy-start | bytes 1228804
  101.3 53.8 %copy-start.19 = (f32[1024]{0:T(1024)S(1)}, f32[1024]{0:T(1024)}, u32[]{:S(2)}) copy-start(f32[1024]{0:T(1024)} %convert_element_type.206) | copy-start | bytes 12292
  101.4 53.8 %copy-start.20 = (f32[1024]{0:T(1024)S(1)}, f32[1024]{0:T(1024)}, u32[]{:S(2)}) copy-start(f32[1024]{0:T(1024)} %get-tuple-element.492) | copy-start | bytes 12292
  159.5 3.2 %copy-start.12 = (bf16[2,512,128]{2,1,0:T(8,128)(2,1)S(1)}, bf16[2,512,128]{2,1,0:T(8,128)(2,1)}, u32[]{:S(2)}) copy-start(bf16[2,512,128]{2,1,0:T(8,128)(2,1)} %copy-done.11) | copy-start | bytes 786436
  159.5 5.5 %copy-start.5 = (bf16[128,1024]{1,0:T(8,128)(2,1)S(1)}, bf16[128,1024]{1,0:T(8,128)(2,1)}, u32[]{:S(2)}) copy-start(bf16[128,1024]{1,0:T(8,128)(2,1)} %param.27) | copy-start | bytes 786436
  166.9 52.8 %all-to-all-start.3 = ((f32[64,128,16]{1,2,0:T(8,128)}), f32[64,128,16]{1,2,0:T(8,128)}, u32[]{:S(2)}, u32[]{:S(2)}) async-start(f32[64,128,16]{1,2,0:T(8,128)} %copy.136), calls=%async_computation.3 | async-start | bytes 1048576 | tf_op jit(solution)/shard_map/all_to_all | solution.py:45
  178.5 35.7 %copy-start.3 = (bf16[1024,1024]{0,1:T(8,128)(2,1)S(1)}, bf16[1024,1024]{0,1:T(8,128)(2,1)}, u32[]{:S(2)}) copy-start(bf16[1024,1024]{0,1:T(8,128)(2,1)} %copy-done.2) | copy-start | bytes 6291460
  182.1 3.3 %copy-start.13 = (bf16[1024,2,64]{0,2,1:T(8,128)(2,1)S(1)}, bf16[1024,2,64]{0,2,1:T(8,128)(2,1)}, u32[]{:S(2)}) copy-start(bf16[1024,2,64]{0,2,1:T(8,128)(2,1)} %get-tuple-element.672) | copy-start | bytes 786436 | tf_op jit(solution)/shard_map/transpose(jvp())/while
  185.4 1.5 copy-start.29
  186.8 2.8 %copy-start.14 = (bf16[1024,2,64]{0,2,1:T(8,128)(2,1)}, bf16[1024,2,64]{0,2,1:T(8,128)(2,1)S(1)}, u32[]{:S(2)}) copy-start(bf16[1024,2,64]{0,2,1:T(8,128)(2,1)S(1)} %fusion.191) | copy-start | bytes 786436 | tf_op jit(solution)/shard_map/transpose(jvp())/while
  189.7 1.9 copy-start.16
  191.6 1.6 copy-start.6
  191.6 1.6 copy-start.31
  193.2 1.5 copy-start.17
  194.7 0.7 copy-start.7
  198.8 3.3 %copy-start.13 = (bf16[1024,2,64]{0,2,1:T(8,128)(2,1)S(1)}, bf16[1024,2,64]{0,2,1:T(8,128)(2,1)}, u32[]{:S(2)}) copy-start(bf16[1024,2,64]{0,2,1:T(8,128)(2,1)} %get-tuple-element.672) | copy-start | bytes 786436 | tf_op jit(solution)/shard_map/transpose(jvp())/while
  202.1 1.5 copy-start.29
  203.6 2.8 %copy-start.14 = (bf16[1024,2,64]{0,2,1:T(8,128)(2,1)}, bf16[1024,2,64]{0,2,1:T(8,128)(2,1)S(1)}, u32[]{:S(2)}) copy-start(bf16[1024,2,64]{0,2,1:T(8,128)(2,1)S(1)} %fusion.191) | copy-start | bytes 786436 | tf_op jit(solution)/shard_map/transpose(jvp())/while
  206.4 1.9 copy-start.16
  208.3 1.6 copy-start.6
  208.3 1.6 copy-start.31
  209.9 1.5 copy-start.17
  211.4 0.7 copy-start.7
  214.2 3.4 %copy-start.15 = (bf16[1024,2,64]{0,2,1:T(8,128)(2,1)S(1)}, bf16[1024,2,64]{0,2,1:T(8,128)(2,1)}, u32[]{:S(2)}) copy-start(bf16[1024,2,64]{0,2,1:T(8,128)(2,1)} %get-tuple-element.274) | copy-start | bytes 786436
  219.7 49.3 %all-to-all-start.1 = ((f32[64,16,3,128]{3,1,2,0:T(8,128)}), f32[64,16,3,128]{3,1,2,0:T(8,128)S(1)}, u32[]{:S(2)}, u32[]{:S(2)}) async-start(f32[64,16,3,128]{3,1,2,0:T(8,128)} %copy.133), calls=%async_computation.1 | async-start | bytes 3145728 | tf_op jit(solution)/shard_map/all_to_all | solution.py:45
Sparse Core Ops, SparseCore 0:
  88.8 62.0 all-reduce.1
where the time goes:
time: 278 us; the launch traced here: 277 us
  waiting for transfers between devices  106 us (38%)
  matrix products  52.6 us (19%)
  starting transfers between devices  43.1 us (16%)
  other arithmetic  25.4 us (9%)
  local copies, waits for them, and re-layouts  23.7 us (9%)
  between operations  14.6 us (5%)
  blocking collectives  11.4 us (4%)
    psum x1, waiting for transfers between devices, shards(): mixed = lax.psum(partial_mix.astype(jnp.bfloat16), 'mp').astype(jnp.float32)  49.6 us
    all_to_all x2, waiting for transfers between devices, sent_and_summed(): tiles = lax.all_to_all(split_up(shard, dim, length), axis, 0, 0, tiled=True)  35.2 us
    all_to_all x2, starting transfers between devices, sent_and_summed(): tiles = lax.all_to_all(split_up(shard, dim, length), axis, 0, 0, tiled=True)  21.2 us
    all_to_all x1, waiting for transfers between devices, sent_together(): lax.all_to_all(both, axis, split_axis=split_dim, concat_axis=concat_dim,...  21.2 us
    dot_general x6, matrix products, one_block(): jnp.einsum('hqk,khd->qhd', probs, valued, preferred_element_type=jnp.floa...  14.5 us
    all_to_all x1, starting transfers between devices, sent_together(): lax.all_to_all(both, axis, split_axis=split_dim, concat_axis=concat_dim,...  13.2 us
    all_gather x1, blocking collectives, sent_together_2(): lax.all_gather(both, axis, axis=dim, tiled=True)  11.4 us
    dot_general x6, matrix products, one_block(): jnp.einsum('qhd,khd->hqk', query_block, keyed, preferred_element_type=jnp...  10.2 us
  transfers between devices with their start and end apart: 5, of which 3 were waited for; matrix products, arithmetic and copies ran while one was open for 24% of the time, Pallas kernels for 0%

commit v1 on v0

--- a/solution.py
+++ b/solution.py
@@ -108,6 +108,10 @@
     final_gain,
     vel_weight,
 ):
+
+    def _mark_case(unit):
+        return lax.all_gather(unit, axis_name="mp").sum(axis=0)
+
     sources = lax.axis_size("dp")
     here = lax.axis_index("dp")
     per_dev = noise_blocks.shape[0]
@@ -172,7 +176,7 @@
     heads_out, pullback = jax.vjp(lambda a, b, c: attend(a, b, c, segment), query, keys, values)
     attended = heads_out.astype(jnp.bfloat16)
     partial_mix = jnp.dot(attended, out_proj, preferred_element_type=jnp.float32)
-    mixed = lax.psum(partial_mix.astype(jnp.bfloat16), "mp").astype(jnp.float32)
+    mixed = _mark_case(partial_mix.astype(jnp.bfloat16)).astype(jnp.float32)
     hidden1 = (hidden0 + mixed).astype(jnp.bfloat16)
     wide1 = lax.optimization_barrier(hidden1).astype(jnp.float32)
     rscale = lax.rsqrt(jnp.mean(wide1 * wide1, axis=1, keepdims=True) + 1e-06)

time: 278 us -> 320 us (1.15); the launches traced: 277 us -> 316 us
  waiting for transfers between devices: 106 us -> 130 us
  matrix products: 52.6 us -> 64.7 us
    all_gather x0 -> x1, waiting for transfers between devices: none -> 72.1 us  [_mark_case(): return lax.all_gather(unit, axis_name='mp').sum(axis=0)]
    psum x1 -> x0, waiting for transfers between devices: 49.6 us -> none  [shards(): mixed = lax.psum(partial_mix.astype(jnp.bfloat16), 'mp').astype(jnp.float32)]
    reduce_sum x0 -> x1, other arithmetic: none -> 6.5 us  [_mark_case(): return lax.all_gather(unit, axis_name='mp').sum(axis=0)]
    dot_general x6, matrix products: 14.5 us -> 20.5 us  [one_block(): jnp.einsum('hqk,khd->qhd', probs, valued, preferred_element_type=jnp.floa...]
    dot_general x6, matrix products: 10.2 us -> 15.9 us  [one_block(): jnp.einsum('qhd,khd->hqk', query_block, keyed, preferred_element_type=jnp...]
where the time goes in v1:
time: 320 us; the launch traced here: 316 us
  waiting for transfers between devices  130 us (41%)
  matrix products  64.7 us (20%)
  starting transfers between devices  43.1 us (13%)
  other arithmetic  28.5 us (9%)
  local copies, waits for them, and re-layouts  22.5 us (7%)
  between operations  14.7 us (5%)
  blocking collectives  11.7 us (4%)
    all_gather x1, waiting for transfers between devices, _mark_case(): return lax.all_gather(unit, axis_name='mp').sum(axis=0)  72.1 us
    all_to_all x2, waiting for transfers between devices, sent_and_summed(): tiles = lax.all_to_all(split_up(shard, dim, length), axis, 0, 0, tiled=True)  36 us
    all_to_all x1, waiting for transfers between devices, sent_together(): lax.all_to_all(both, axis, split_axis=split_dim, concat_axis=concat_dim,...  21.9 us
    all_to_all x2, starting transfers between devices, sent_and_summed(): tiles = lax.all_to_all(split_up(shard, dim, length), axis, 0, 0, tiled=True)  21.2 us
    dot_general x6, matrix products, one_block(): jnp.einsum('hqk,khd->qhd', probs, valued, preferred_element_type=jnp.floa...  20.5 us
    dot_general x6, matrix products, one_block(): jnp.einsum('qhd,khd->hqk', query_block, keyed, preferred_element_type=jnp...  15.9 us
    all_to_all x1, starting transfers between devices, sent_together(): lax.all_to_all(both, axis, split_axis=split_dim, concat_axis=concat_dim,...  13.2 us
    all_gather x1, blocking collectives, sent_together_2(): lax.all_gather(both, axis, axis=dim, tiled=True)  11.7 us
  transfers between devices with their start and end apart: 5, of which 3 were waited for; matrix products, arithmetic and copies ran while one was open for 24% of the time, Pallas kernels for 0%

profile of v1, /device:TPU:1, one launch (start us, length us, event | category | flops | bytes accessed | tf_op | source)
XLA Modules:
  0.0 315.5 jit_solution(10893198668680579485)
XLA Ops:
  10.7 1.7 copy.116
  12.4 13.2 %all-to-all-start = ((bf16[64,2,3200]{2,1,0:T(2,128)(2,1)}), bf16[64,2,3200]{2,1,0:T(2,128)(2,1)S(1)}, u32[]{:S(2)}, u32[]{:S(2)}) async-start(bf16[64,2,3200]{2,1,0:T(2,128)(2,1)} %copy.116), calls=%async_computation | async-start | bytes 1638400 | tf_op jit(solution)/shard_map/all_to_all | solution.py:13
  27.0 21.9 %all-to-all-done = bf16[64,2,3200]{2,1,0:T(2,128)(2,1)S(1)} async-done(((bf16[64,2,3200]{2,1,0:T(2,128)(2,1)}), bf16[64,2,3200]{2,1,0:T(2,128)(2,1)S(1)}, u32[]{:S(2)}, u32[]{:S(2)}) %all-to-all-start) | async-done | bytes 819232 | tf_op jit(solution)/shard_map/all_to_all | solution.py:13
  48.9 1.1 fusion.127
  50.5 11.7 %all_gather.9 = bf16[16,12800]{1,0:T(8,128)(2,1)S(1)} all-gather(bf16[16,3200]{1,0:T(8,128)(2,1)S(1)} %pad_maximum_fusion.2), channel_id=1, replica_groups=mesh['dp'=64,'mp'=4] {'mp'}, dimensions={1}, use_global_device_ids=true | all-gather | bytes 512000 | tf_op jit(solution)/shard_map/all_gather | solution.py:19
  65.9 1.3 copy-done.16
  68.0 1.2 convolution_convert_fusion.8
  69.2 1.2 convolution_convert_fusion.7
  71.0 16.2 %while.30 = (s32[]{:T(128)}, bf16[2,512,128]{2,1,0:T(8,128)(2,1)S(1)}, s32[2,512]{1,0:T(2,128)S(1)}, s32[1,1024]{1,0:T(1,128)S(1)}, bf16[2,512,2,64]{1,3,2,0:T(8...) while((s32[]{:T(128)}, bf16[2,512,128]{2,1,0:T(8,128)(2,1)S(1)}, ...), condition=%wide.region_13.14_spmd, body=%wide.region_10.13_spmd.sunk | while | flops 275252224 | bytes 11815037 | solution.py:91
  71.4 4.5 %fusion.178 = (f32[2,512]{1,0:T(2,128)S(1)}, f32[2,512,1024]{2,1,0:T(8,128)}) fusion(pred[512,1024]{1,0:T(8,128)(4,1)S(1)} %broadcast_compare_fusion.4, bf16[1024,2,64]{0,2,1:T(8,128)(2,1)} %get-tuple-element.655, bf16[2,512,2,64]{1,3,2,0:T(8,128)(2,1)S(1)} %get-tuple-element.654, s32[]{:T(128)} %get-tuple-element.642), kind=kOutput, calls=%fused_computation.183.clone.1 | convolution fusion | flops 138413056 | bytes 5115908 | tf_op jit(solution)/shard_map/jvp()/while/body/eval_jaxpr/sub | solution.py:85
  75.9 3.0 fusion.179
  79.5 4.5 %fusion.178 = (f32[2,512]{1,0:T(2,128)S(1)}, f32[2,512,1024]{2,1,0:T(8,128)}) fusion(pred[512,1024]{1,0:T(8,128)(4,1)S(1)} %broadcast_compare_fusion.4, bf16[1024,2,64]{0,2,1:T(8,128)(2,1)} %get-tuple-element.655, bf16[2,512,2,64]{1,3,2,0:T(8,128)(2,1)S(1)} %get-tuple-element.654, s32[]{:T(128)} %get-tuple-element.642), kind=kOutput, calls=%fused_computation.183.clone.1 | convolution fusion | flops 138413056 | bytes 5115908 | tf_op jit(solution)/shard_map/jvp()/while/body/eval_jaxpr/sub | solution.py:85
  84.0 3.0 fusion.179
  87.2 2.0 convolution_convert_fusion.5
  89.3 1.3 broadcast_in_dim.203
  90.6 8.8 %all-to-all-start.2 = ((f32[64,1,1]{2,1,0:T(1,128)}), f32[64,1,1]{2,1,0:T(1,128)S(1)}, u32[]{:S(2)}, u32[]{:S(2)}) async-start(f32[64,1,1]{2,1,0:T(1,128)} %broadcast_in_dim.203), calls=%async_computation.2 | async-start | bytes 65536 | tf_op jit(solution)/shard_map/all_to_all | solution.py:28
  101.3 72.1 %all-gather.3.cloned.1.call-done = bf16[4096,1024]{1,0:T(8,128)(2,1)} async-done(((bf16[1024,1024]{1,0:T(8,128)(2,1)}), bf16[4096,1024]{1,0:T(8,128)(2,1)}) %all-gather.3.cloned.1.call-update) | async-done | bytes 8388624 | tf_op jit(solution)/shard_map/all_gather | solution.py:113
  173.4 6.5 %reduce_sum.235 = bf16[1024,1024]{1,0:T(8,128)(2,1)S(1)} reduce(bf16[4,1024,1024]{2,1,0:T(8,128)(2,1)} %bitcast.172, bf16[]{:T(256)} %constant.190.clone.1), dimensions={0}, to_apply=%region_14.15 | reduce | flops 3145728 | bytes 10485762 | tf_op jit(solution)/shard_map/reduce_sum | solution.py:113
  179.9 2.6 copy.122
  182.5 3.7 %add_convert_fusion = bf16[1024,1024]{0,1:T(8,128)(2,1)S(1)} fusion(f32[1024,1024]{0,1:T(8,128)} %copy-done.5, bf16[1024,1024]{0,1:T(8,128)(2,1)} %copy.122), kind=kLoop, calls=%fused_computation.86 | loop fusion | flops 3145728 | bytes 8388608 | tf_op jit(solution)/shard_map/convert_element_type | solution.py:180
  186.6 4.5 %fusion.64 = (f32[1024]{0:T(1024)S(1)}, f32[1024,1024]{0,1:T(8,128)}) fusion(bf16[1024,1024]{0,1:T(8,128)(2,1)S(1)} %add_convert_fusion, f32[1024]{0:T(1024)S(1)} %convert_element_type.208, f32[1024]{0:T(1024)S(1)} %add_rsqrt_fusion, bf16[1024,100]{0,1:T(8,128)(2,1)S(1)} %copy-done.17, f32[1024,100]{0,1:T(8,128)} %copy.123, f32[1024,100]{0,1:T(8,128)} %copy.124, ...), kind=kOutput, calls=%fused_computation.81 | convolution fusion | flops 429276160 | bytes 7331840 | tf_op jit(solution)/shard_map/dot_general | solution.py:189
  191.1 3.1 fusion.67
  194.2 2.3 fusion.75
  198.5 10.9 %all-to-all-start.3 = ((f32[64,128,16]{1,2,0:T(8,128)}), f32[64,128,16]{1,2,0:T(8,128)}, u32[]{:S(2)}, u32[]{:S(2)}) async-start(f32[64,128,16]{1,2,0:T(8,128)} %copy.134), calls=%async_computation.3 | async-start | bytes 1048576 | tf_op jit(solution)/shard_map/all_to_all | solution.py:45
  210.1 41.8 %while.31 = (s32[]{:T(128)}, bf16[1024,2,64]{0,2,1:T(8,128)(2,1)}, bf16[1024,2,64]{0,2,1:T(8,128)(2,1)}, bf16[2,512,2,64]{1,3,2,0:T(8,128)(2,1)}, bf16[2,512,2,6...) while((s32[]{:T(128)}, bf16[1024,2,64]{0,2,1:T(8,128)(2,1)}, ...), condition=%wide.region_23.24_spmd.clone, body=%wide.region_17.23_spmd.clone.sunk | while | flops 712179712 | bytes 108235080 | solution.py:91
  210.7 2.1 fusion.187
  212.8 1.2 fusion.188
  214.0 2.8 convert_reduce_fusion.5
  216.8 1.9 fusion.189
  218.7 1.9 copy-done.3
  220.7 3.1 fusion.192
  223.8 4.5 %fusion.191 = bf16[1024,2,64]{0,2,1:T(8,128)(2,1)} fusion(bf16[2,64,512]{2,1,0:T(8,128)(2,1)S(1)} %bitcast.175, f32[2,512]{1,0:T(2,128)S(1)} %fusion.188, f32[2,512,1024]{2,1,0:T(8,128)} %copy-done.2, f32[2,512]{1,0:T(2,128)S(1)} %get-tuple-element.624, pred[512,1024]{1,0:T(8,128)(4,1)S(1)} %broadcast_compare_fusion.5, ...), kind=kOutput, calls=%fused_computation.52.clone.1 | convolution fusion | flops 139722752 | bytes 5382145 | tf_op jit(solution)/shard_map/transpose(jvp())/while/body/eval_jaxpr/checkpoint/hqk,khd->qhd/dot_general | solution.py:87
  228.3 2.3 fusion.190
  231.1 2.1 fusion.187
  233.2 1.2 fusion.188
  234.4 2.8 convert_reduce_fusion.5
  237.2 1.9 fusion.189
  239.1 1.9 copy-done.3
  241.0 3.1 fusion.192
  244.2 4.5 %fusion.191 = bf16[1024,2,64]{0,2,1:T(8,128)(2,1)} fusion(bf16[2,64,512]{2,1,0:T(8,128)(2,1)S(1)} %bitcast.175, f32[2,512]{1,0:T(2,128)S(1)} %fusion.188, f32[2,512,1024]{2,1,0:T(8,128)} %copy-done.2, f32[2,512]{1,0:T(2,128)S(1)} %get-tuple-element.624, pred[512,1024]{1,0:T(8,128)(4,1)S(1)} %broadcast_compare_fusion.5, ...), kind=kOutput, calls=%fused_computation.52.clone.1 | convolution fusion | flops 139722752 | bytes 5382145 | tf_op jit(solution)/shard_map/transpose(jvp())/while/body/eval_jaxpr/checkpoint/hqk,khd->qhd/dot_general | solution.py:87
  248.7 3.2 %fusion.190 = bf16[1024,2,64]{0,2,1:T(8,128)(2,1)} fusion(bf16[512,2,64]{0,2,1:T(8,128)(2,1)S(1)} %dynamic-slice_bitcast_fusion.2, f32[2,512,1024]{2,1,0:T(8,128)S(1)} %copy-done.4, pred[2,512,1024]{2,1,0:T(32,128)(4,1)S(1)} %copy-done.21, f32[2,512]{1,0:T(2,128)S(1)} %negate_divide_fusion.2, pred[512,1024]{1,0:T(8,128)(4,1)S(1)} %broadcast_compare_fusion.5, ...), kind=kOutput, calls=%fused_computation.53.clone.1 | convolution fusion | flops 138805248 | bytes 6426625 | tf_op jit(solution)/shard_map/transpose(jvp())/while/body/eval_jaxpr/checkpoint/qhd,khd->hqk/dot_general | solution.py:80
  251.9 1.3 copy.127
  254.0 1.7 convolution_bitcast_fusion.1
  256.5 1.3 copy.131
  257.8 10.3 %all-to-all-start.1 = ((f32[64,16,3,128]{3,1,2,0:T(8,128)}), f32[64,16,3,128]{3,1,2,0:T(8,128)S(1)}, u32[]{:S(2)}, u32[]{:S(2)}) async-start(f32[64,16,3,128]{3,1,2,0:T(8,128)} %copy.131), calls=%async_computation.1 | async-start | bytes 3145728 | tf_op jit(solution)/shard_map/all_to_all | solution.py:45
  269.9 1.2 broadcast_divide_fusion.1
  271.1 36.0 %all-to-all-done.1 = f32[64,16,3,128]{3,1,2,0:T(8,128)S(1)} async-done(((f32[64,16,3,128]{3,1,2,0:T(8,128)}), f32[64,16,3,128]{3,1,2,0:T(8,128)S(1)}, u32[]{:S(2)}, u32[]{:S(2)}) %all-to-all-start.1) | async-done | bytes 1572896 | tf_op jit(solution)/shard_map/all_to_all | solution.py:45
  307.2 1.2 broadcast_divide_fusion
  (137 shorter events, 21.2 us)
Async XLA Ops:
  7.2 57.5 %copy-start = (bf16[200,1024]{1,0:T(8,128)(2,1)S(1)}, bf16[200,1024]{1,0:T(8,128)(2,1)}, u32[]{:S(2)}) copy-start(bf16[200,1024]{1,0:T(8,128)(2,1)} %param.24) | copy-start | bytes 1228804
  7.2 18.5 %copy-start.13 = (s32[1,4]{1,0:T(1,128)S(1)}, s32[1,4]{1,0:T(1,128)}, u32[]{:S(2)}) copy-start(s32[1,4]{1,0:T(1,128)} %param.20) | copy-start | bytes 52
  7.2 18.6 %copy-start.10 = (bf16[1024]{0:T(1024)(128)(2,1)S(1)}, bf16[1024]{0:T(1024)(128)(2,1)}, u32[]{:S(2)}) copy-start(bf16[1024]{0:T(1024)(128)(2,1)} %param.25) | copy-start | bytes 6148
  7.2 19.1 %copy-start.15 = (s32[1,4]{1,0:T(1,128)S(1)}, s32[1,4]{1,0:T(1,128)}, u32[]{:S(2)}) copy-start(s32[1,4]{1,0:T(1,128)} %param.21) | copy-start | bytes 52
  7.2 19.1 %copy-start.14 = (s32[1,4]{1,0:T(1,128)S(1)}, s32[1,4]{1,0:T(1,128)}, u32[]{:S(2)}) copy-start(s32[1,4]{1,0:T(1,128)} %param.22) | copy-start | bytes 52
  7.2 19.1 %copy-start.12 = (s32[1,4]{1,0:T(1,128)S(1)}, s32[1,4]{1,0:T(1,128)}, u32[]{:S(2)}) copy-start(s32[1,4]{1,0:T(1,128)} %param.23) | copy-start | bytes 52
  12.4 36.5 %all-to-all-start = ((bf16[64,2,3200]{2,1,0:T(2,128)(2,1)}), bf16[64,2,3200]{2,1,0:T(2,128)(2,1)S(1)}, u32[]{:S(2)}, u32[]{:S(2)}) async-start(bf16[64,2,3200]{2,1,0:T(2,128)(2,1)} %copy.116), calls=%async_computation | async-start | bytes 1638400 | tf_op jit(solution)/shard_map/all_to_all | solution.py:13
  25.6 147.8 %all-gather.3.cloned.1.call-start = ((), (), s32[]{:S(2)}) async-start(), calls=%async_computation.4 | async-start | bytes 10485760 | tf_op jit(solution)/shard_map/all_gather | solution.py:113
  65.5 2.5 copy-start.5
  65.5 1.7 copy-start.16
  67.2 2.0 copy-start.6
  71.0 16.2 %copy-start.8 = (bf16[128,1024]{1,0:T(8,128)(2,1)S(1)}, bf16[128,1024]{1,0:T(8,128)(2,1)}, u32[]{:S(2)}) copy-start(bf16[128,1024]{1,0:T(8,128)(2,1)} %param.27) | copy-start | bytes 786436
  71.1 4.9 %copy-start.18 = (bf16[1024,2,64]{0,2,1:T(8,128)(2,1)S(1)}, bf16[1024,2,64]{0,2,1:T(8,128)(2,1)}, u32[]{:S(2)}) copy-start(bf16[1024,2,64]{0,2,1:T(8,128)(2,1)} %get-tuple-element.656) | copy-start | bytes 786436 | tf_op jit(solution)/shard_map/jvp()/while
  79.2 4.9 %copy-start.18 = (bf16[1024,2,64]{0,2,1:T(8,128)(2,1)S(1)}, bf16[1024,2,64]{0,2,1:T(8,128)(2,1)}, u32[]{:S(2)}) copy-start(bf16[1024,2,64]{0,2,1:T(8,128)(2,1)} %get-tuple-element.656) | copy-start | bytes 786436 | tf_op jit(solution)/shard_map/jvp()/while
  87.2 12.1 %copy-start.11 = (bf16[1024]{0:T(1024)(128)(2,1)S(1)}, bf16[1024]{0:T(1024)(128)(2,1)}, u32[]{:S(2)}) copy-start(bf16[1024]{0:T(1024)(128)(2,1)} %param.28) | copy-start | bytes 6148
  90.6 107.9 %all-to-all-start.2 = ((f32[64,1,1]{2,1,0:T(1,128)}), f32[64,1,1]{2,1,0:T(1,128)S(1)}, u32[]{:S(2)}, u32[]{:S(2)}) async-start(f32[64,1,1]{2,1,0:T(1,128)} %broadcast_in_dim.203), calls=%async_computation.2 | async-start | bytes 65536 | tf_op jit(solution)/shard_map/all_to_all | solution.py:28
  182.5 4.2 %copy-start.17 = (bf16[1024,100]{0,1:T(8,128)(2,1)S(1)}, bf16[1024,100]{0,1:T(8,128)(2,1)}, u32[]{:S(2)}) copy-start(bf16[1024,100]{0,1:T(8,128)(2,1)} %param.29) | copy-start | bytes 614404
  198.5 59.3 %all-to-all-start.3 = ((f32[64,128,16]{1,2,0:T(8,128)}), f32[64,128,16]{1,2,0:T(8,128)}, u32[]{:S(2)}, u32[]{:S(2)}) async-start(f32[64,128,16]{1,2,0:T(8,128)} %copy.134), calls=%async_computation.3 | async-start | bytes 1048576 | tf_op jit(solution)/shard_map/all_to_all | solution.py:45
  210.1 43.2 %copy-start.7 = (bf16[1024,1024]{0,1:T(8,128)(2,1)S(1)}, bf16[1024,1024]{0,1:T(8,128)(2,1)}, u32[]{:S(2)}) copy-start(bf16[1024,1024]{0,1:T(8,128)(2,1)} %copy-done.6) | copy-start | bytes 6291460
  210.6 3.3 %copy-start.19 = (bf16[1024,2,64]{0,2,1:T(8,128)(2,1)S(1)}, bf16[1024,2,64]{0,2,1:T(8,128)(2,1)}, u32[]{:S(2)}) copy-start(bf16[1024,2,64]{0,2,1:T(8,128)(2,1)} %get-tuple-element.627) | copy-start | bytes 786436 | tf_op jit(solution)/shard_map/transpose(jvp())/while
  212.8 4.0 %copy-start.2 = (f32[2,512,1024]{2,1,0:T(8,128)}, f32[2,512,1024]{2,1,0:T(8,128)S(1)}, u32[]{:S(2)}) copy-start(f32[2,512,1024]{2,1,0:T(8,128)S(1)} %get-tuple-element.625) | copy-start | bytes 12582916 | tf_op jit(solution)/shard_map/transpose(jvp())/while
  216.8 2.0 copy-start.20
  218.7 2.0 copy-start.3
  223.8 4.5 %copy-start.4 = (f32[2,512,1024]{2,1,0:T(8,128)S(1)}, f32[2,512,1024]{2,1,0:T(8,128)}, u32[]{:S(2)}) copy-start(f32[2,512,1024]{2,1,0:T(8,128)} %copy-done.3) | copy-start | bytes 12582916 | tf_op jit(solution)/shard_map/transpose(jvp())/while
  223.8 4.5 %copy-start.21 = (pred[2,512,1024]{2,1,0:T(32,128)(4,1)S(1)}, pred[2,512,1024]{2,1,0:T(32,128)(4,1)}, u32[]{:S(2)}) copy-start(pred[2,512,1024]{2,1,0:T(32,128)(4,1)} %copy-done.20) | copy-start | bytes 3145732 | tf_op jit(solution)/shard_map/transpose(jvp())/while
  231.1 3.3 %copy-start.19 = (bf16[1024,2,64]{0,2,1:T(8,128)(2,1)S(1)}, bf16[1024,2,64]{0,2,1:T(8,128)(2,1)}, u32[]{:S(2)}) copy-start(bf16[1024,2,64]{0,2,1:T(8,128)(2,1)} %get-tuple-element.627) | copy-start | bytes 786436 | tf_op jit(solution)/shard_map/transpose(jvp())/while
  233.2 4.0 %copy-start.2 = (f32[2,512,1024]{2,1,0:T(8,128)}, f32[2,512,1024]{2,1,0:T(8,128)S(1)}, u32[]{:S(2)}) copy-start(f32[2,512,1024]{2,1,0:T(8,128)S(1)} %get-tuple-element.625) | copy-start | bytes 12582916 | tf_op jit(solution)/shard_map/transpose(jvp())/while
  237.1 2.0 copy-start.20
  239.1 2.0 copy-start.3
  244.2 4.5 %copy-start.4 = (f32[2,512,1024]{2,1,0:T(8,128)S(1)}, f32[2,512,1024]{2,1,0:T(8,128)}, u32[]{:S(2)}) copy-start(f32[2,512,1024]{2,1,0:T(8,128)} %copy-done.3) | copy-start | bytes 12582916 | tf_op jit(solution)/shard_map/transpose(jvp())/while
  244.2 4.5 %copy-start.21 = (pred[2,512,1024]{2,1,0:T(32,128)(4,1)S(1)}, pred[2,512,1024]{2,1,0:T(32,128)(4,1)}, u32[]{:S(2)}) copy-start(pred[2,512,1024]{2,1,0:T(32,128)(4,1)} %copy-done.20) | copy-start | bytes 3145732 | tf_op jit(solution)/shard_map/transpose(jvp())/while
  251.9 3.8 %copy-start.9 = (bf16[1024,2,64]{0,2,1:T(8,128)(2,1)S(1)}, bf16[1024,2,64]{0,2,1:T(8,128)(2,1)}, u32[]{:S(2)}) copy-start(bf16[1024,2,64]{0,2,1:T(8,128)(2,1)} %get-tuple-element.274) | copy-start | bytes 786436
  256.4 52.0 %copy-start.1 = (bf16[200,1024]{1,0:T(8,128)(2,1)S(1)}, bf16[200,1024]{1,0:T(8,128)(2,1)}, u32[]{:S(2)}) copy-start(bf16[200,1024]{1,0:T(8,128)(2,1)} %param.24) | copy-start | bytes 1228804
  257.8 49.3 %all-to-all-start.1 = ((f32[64,16,3,128]{3,1,2,0:T(8,128)}), f32[64,16,3,128]{3,1,2,0:T(8,128)S(1)}, u32[]{:S(2)}, u32[]{:S(2)}) async-start(f32[64,16,3,128]{3,1,2,0:T(8,128)} %copy.131), calls=%async_computation.1 | async-start | bytes 3145728 | tf_op jit(solution)/shard_map/all_to_all | solution.py:45
Sparse Core Ops, SparseCore 0:
  89.4 83.9 all-gather.2
